TPU v7x, 256 devices: a whole 4x4x8 slice. The times are simulated.
256 devices in a mesh: ctx: 16 (over x, y), head: 16 (over z, core).
Axes of the slice: x: 4, y: 4, z: 8, core: 2. Of those that a mesh axis runs over, the one named last changes fastest.
Arguments:
- tokens: bfloat16 [16384, 4096], P('ctx', 'head'), may hold values from -6 to 6
- doc_ids: int32 [16384], P('ctx'), may hold values from 0 to 7, never falling along the last dimension, each value on 1 to 8192 neighbouring positions
- w_feat: bfloat16 [4096, 1024], P(None, 'head'), may hold values from -0.09375 to 0.09375
- w_value: bfloat16 [4096, 4096], P(None, 'head'), may hold values from -0.09375 to 0.09375
- w_window: bfloat16 [4096, 8192], P(None, 'head'), may hold values from -4 to 4
- w_out: bfloat16 [4096, 4096], P('head'), may hold values from -0.09375 to 0.09375
Outputs:
- layer_out: bfloat16 [16384, 4096], P('ctx', 'head')
Inputs may be any that keep to these rules, and one draw needn't show every extreme that they name: `doc_ids`: document ids never fall along the sequence; each of the 8 documents has 1 to 8192 tokens, and one has exactly 8192.
All inputs are finite; a program needn't handle non-finite values.
Results may differ from a plain program's by a relative error of at most 0.019.
Values may be sent and summed in bfloat16 or wider, within the bound.
A program may use at most 128 MiB of HBM per device.

v0:
```python
import jax
import jax.numpy as jnp
from jax import lax
from jax.sharding import PartitionSpec as P

HEAD_DIM = 128
FEAT = 16
WIN = 64


def entering(x, axis, join, neutral):
    place = lax.axis_index(axis)
    gathered = jax.tree.map(
        lambda a, kind: lax.all_gather(a.astype(kind), axis), x, (jnp.bfloat16, jnp.bfloat16)
    )
    state = jax.tree.map(lambda a, e: jnp.zeros_like(a) + jnp.asarray(e, a.dtype), x, neutral)

    def one(step, state):
        return join(
            state,
            jax.tree.map(
                lambda a, own: lax.dynamic_index_in_dim(a, step, 0, False).astype(own.dtype),
                gathered,
                x,
            ),
        )

    return lax.fori_loop(0, place, one, state)


def shifted(x, axis, by):
    devices = lax.axis_size(axis)
    pairs = [(i, i + by) for i in range(devices) if 0 <= i + by < devices]
    return lax.ppermute(x, axis, pairs)


def feature_map(projected):
    widened = projected.astype(jnp.float32)
    products = widened[..., :, None] * widened[..., None, :]
    products = products.reshape(widened.shape[:-1] + (FEAT * FEAT,))
    constant_term = jnp.ones(widened.shape[:-1] + (1,), jnp.float32)
    return jnp.concatenate(
        [constant_term, widened * FEAT ** (-0.25), products * (2.0 * FEAT) ** (-0.5)], -1
    ).astype(jnp.bfloat16)


def join_states(earlier, later):
    early_state, early_doc = earlier
    late_state, late_doc = later
    empty_late = late_doc[0] < 0.0
    matched = early_doc[0] == late_doc[0]
    joined = late_state + jnp.where(matched, early_state, jnp.zeros_like(early_state))
    return (jnp.where(empty_late, early_state, joined), jnp.where(empty_late, early_doc, late_doc))


def shards(tokens, doc_ids, w_feat, w_value, w_window, w_out):
    tok_rows = tokens.shape[0]
    head_count = w_value.shape[1] // HEAD_DIM
    highest = lax.Precision.HIGHEST
    zero_sums = (
        jnp.zeros((tok_rows, w_feat.shape[1]), jnp.float32),
        jnp.zeros((tok_rows, w_value.shape[1]), jnp.float32),
        jnp.zeros((tok_rows, w_window.shape[1]), jnp.float32),
    )
    column_piece = lax.all_gather(tokens, "head", axis=1, tiled=True)
    updated = []
    for running, weight in zip(zero_sums, (w_feat, w_value, w_window)):
        updated.append(jnp.dot(column_piece, weight, preferred_element_type=jnp.float32))
    feat_sum, value_sum, window_sum = tuple(updated)
    features = feat_sum.astype(jnp.bfloat16).reshape(tok_rows, head_count, 2 * FEAT)
    phi_query = feature_map(features[..., :FEAT])
    phi_key = feature_map(features[..., FEAT:])
    values_here = value_sum.astype(jnp.bfloat16).reshape(tok_rows, head_count, HEAD_DIM)
    window_proj = window_sum.astype(jnp.bfloat16).reshape(tok_rows, head_count, 2, HEAD_DIM)
    win_query = window_proj[:, :, 0]
    win_key = window_proj[:, :, 1]
    doc_float = doc_ids.astype(jnp.float32)
    positions = jnp.arange(tok_rows)
    allowed = (
        (doc_float[:, None] == doc_float[None, :]) & (positions[:, None] >= positions[None, :])
    ).astype(jnp.float32)
    scores = (
        jnp.einsum("thp,shp->hts", phi_query, phi_key, preferred_element_type=jnp.float32)
        * allowed[None]
    ).astype(jnp.bfloat16)
    inner = jnp.einsum("hts,shd->thd", scores, values_here, preferred_element_type=jnp.float32)
    keeps = doc_float == doc_float[-1]
    kept_keys = jnp.where(keeps[:, None, None], phi_key, jnp.zeros_like(phi_key))
    local_state = jnp.einsum(
        "shp,shd->hpd", kept_keys, values_here, preferred_element_type=jnp.float32
    )
    last_here = doc_float[tok_rows - 1 :]
    empty_state = jnp.zeros_like(local_state)
    incoming, in_doc = entering(
        (local_state, last_here),
        "ctx",
        join_states,
        (empty_state, jnp.full((1,), -1.0, jnp.float32)),
    )
    uses = doc_float == in_doc[0]
    carried = jnp.einsum("thp,hpd->thd", phi_query.astype(jnp.float32), incoming, precision=highest)
    linear_out = inner + jnp.where(uses[:, None, None], carried, jnp.zeros_like(carried))
    mean_square = jnp.mean(linear_out * linear_out, -1, keepdims=True)
    normed = linear_out * lax.rsqrt(mean_square + 1e-05)
    tail_key, tail_value, tail_doc = shifted(
        (
            win_key[tok_rows - WIN :],
            values_here[tok_rows - WIN :],
            (doc_float[tok_rows - WIN :] + 1.0).astype(jnp.bfloat16),
        ),
        "ctx",
        1,
    )
    keys_all = jnp.concatenate([tail_key, win_key], 0)
    values_cat = jnp.concatenate([tail_value, values_here], 0)
    docs_cat = jnp.concatenate([tail_doc.astype(jnp.float32) - 1.0, doc_float], 0)
    key_pos = jnp.arange(WIN + tok_rows)
    within = (
        (key_pos[None, :] > positions[:, None])
        & (key_pos[None, :] <= positions[:, None] + WIN)
        & (docs_cat[None, :] == doc_float[:, None])
    )
    logits = jnp.einsum(
        "thd,shd->hts", win_query, keys_all, preferred_element_type=jnp.float32
    ) * HEAD_DIM ** (-0.5)
    logits = jnp.where(within[None], logits, -1e30)
    top_logit = jnp.max(logits, -1, keepdims=True)
    weights = jnp.exp(logits - top_logit) * within[None].astype(jnp.float32)
    probs = (weights / jnp.sum(weights, -1, keepdims=True)).astype(jnp.bfloat16)
    window_out = jnp.einsum("hts,shd->thd", probs, values_cat, preferred_element_type=jnp.float32)
    mixed = (normed + window_out).astype(jnp.bfloat16).reshape(tok_rows, head_count * HEAD_DIM)
    summed = lax.psum_scatter(
        lax.dot_general(
            w_out, mixed, (((0,), (1,)), ((), ())), preferred_element_type=jnp.float32
        ).astype(jnp.bfloat16),
        "head",
        scatter_dimension=0,
        tiled=True,
    ).astype(jnp.float32)
    return summed.T.astype(jnp.bfloat16)


def solution(mesh):
    return jax.shard_map(
        shards,
        mesh=mesh,
        in_specs=(
            P("ctx", "head"),
            P("ctx"),
            P(None, "head"),
            P(None, "head"),
            P(None, "head"),
            P("head", None),
        ),
        out_specs=P("ctx", "head"),
        check_vma=False,
    )
```

profile of v0, /device:TPU:2, one launch (start us, length us, event | category | flops | bytes accessed | tf_op | source)
XLA Modules:
  0.0 281.5 jit_solution(10411707166912773014)
XLA Ops:
  8.6 1.2 dynamic-slice
  9.9 1.3 dynamic-update-slice
  11.2 3.5 %collective-permute-start.1 = (bf16[64]{0:T(256)(128)(2,1)S(1)}, bf16[64]{0:T(256)(128)(2,1)S(1)}, u32[]{:S(2)}, u32[]{:S(2)}) collective-permute-start(bf16[64]{0:T(256)(128)(2,1)S(1)} %add_convert_fusion), channel_id=1, source_target_pairs={{0,16},{16,32},{32,48},{48,64},{64,80},{80,96},{96,112},{112,128},... | collective-permute-start | bytes 392 | tf_op jit(solution)/shard_map/ppermute | solution.py:34
  14.7 33.2 %all-reduce = bf16[16]{0:T(256)(128)(2,1)S(1)} all-reduce(bf16[16]{0:T(256)(128)(2,1)S(1)} %dynamic-update-slice), channel_id=2, replica_groups=mesh['ctx'=16,'head'=16] {'ctx'}, use_global_device_ids=true, to_apply=%add | all-reduce | flops 16 | bytes 64
  48.6 1.3 broadcast_compare_fusion.1
  49.9 2.5 fusion.12
  52.4 23.7 %all-gather.5.cloned.1.call-done = bf16[1024,4096]{1,0:T(8,128)(2,1)} async-done(((bf16[1024,256]{1,0:T(8,128)(2,1)}), bf16[1024,4096]{1,0:T(8,128)(2,1)}) %all-gather.5.cloned.1.call-update) | async-done | bytes 8388624 | tf_op jit(solution)/shard_map/all_gather | solution.py:65
  76.1 6.2 %convolution_convert_fusion.3 = bf16[1024,64]{0,1:T(8,128)(2,1)S(1)} fusion(bf16[1024,4096]{1,0:T(8,128)(2,1)} %all-gather.5.cloned.1.call-done, bf16[4096,64]{0,1:T(8,128)(2,1)S(1)} %copy-done.6), kind=kOutput, calls=%fused_computation.36 | convolution fusion | flops 536936448 | bytes 9043968 | tf_op jit(solution)/shard_map/dot_general | solution.py:68
  82.9 1.0 copy-done.11
  83.9 2.3 convolution_convert_fusion.1
  86.3 0.8 copy-done.5
  87.0 1.2 convolution_convert_fusion.2
  88.4 3.5 %fusion.6 = (pred[1024,1088]{0,1:T(8,128)(4,1)}, f32[1024,1088]{0,1:T(8,128)}) fusion(f32[1024]{0:T(1024)S(1)} %convert_element_type.84, s32[1024]{0:T(1024)S(1)} %iota_add_fusion, f32[1088]{0:T(1024)S(1)} %pad_maximum_fusion.12), kind=kLoop, calls=%fused_computation.15 | loop fusion | flops 6684672 | bytes 5583104 | tf_op jit(solution)/shard_map/and | solution.py:119
  92.0 7.3 %convolution_convert_fusion = bf16[1024,512]{0,1:T(8,128)(2,1)S(1)} fusion(bf16[1024,4096]{1,0:T(8,128)(2,1)} %all-gather.5.cloned.1.call-done, bf16[4096,512]{1,0:T(8,128)(2,1)S(1)} %copy-done.10), kind=kOutput, calls=%fused_computation.26 | convolution fusion | flops 4295491584 | bytes 13631488 | tf_op jit(solution)/shard_map/dot_general | solution.py:68
  99.3 1.0 copy-done.8
  100.5 3.4 %collective-permute-start.2 = (bf16[64,2,128]{2,0,1:T(8,128)(2,1)S(1)}, bf16[64,2,128]{2,0,1:T(8,128)(2,1)S(1)}, u32[]{:S(2)}, u32[]{:S(2)}) collective-permute-start(bf16[64,2,128]{2,0,1:T(8,128)(2,1)S(1)} %bitcast.88), channel_id=1, source_target_pairs={{0,16},{16,32},{32,48},{48,64},{64,80},{80,96},{96,112},{112,128},... | collective-permute-start | bytes 98312 | tf_op jit(solution)/shard_map/ppermute | solution.py:34
  103.9 0.8 copy_bitcast_fusion.1
  104.7 3.6 %collective-permute-start = (bf16[64,2,128]{2,0,1:T(8,128)(2,1)S(1)}, bf16[64,2,128]{2,0,1:T(8,128)(2,1)}, u32[]{:S(2)}, u32[]{:S(2)}) collective-permute-start(bf16[64,2,128]{2,0,1:T(8,128)(2,1)S(1)} %copy_bitcast_fusion.1), channel_id=1, source_target_pairs={{0,16},{16,32},{32,48},{48,64},{64,80},{80,96},{96,112},{112,128},... | collective-permute-start | bytes 98312 | tf_op jit(solution)/shard_map/ppermute | solution.py:34
  108.2 2.0 copy_bitcast_fusion
  110.2 7.8 %fusion.9 = f32[2,128,1024]{2,1,0:T(8,128)} fusion(f32[1024,1024]{1,0:T(8,128)} %fusion.12, bf16[1024,2,256]{0,2,1:T(8,128)(2,1)} %bitcast.81, bf16[1024,2,16]{0,2,1:T(8,128)(2,1)S(1)} %get-tuple-element.54, bf16[1024,2,256]{0,2,1:T(8,128)(2,1)S(1)} %bitcast.78, bf16[1024,2,16]{0,2,1:T(8,128)(2,1)S(1)} %get-tuple-element.53, ...), kind=kOutput, calls=%fused_computation.18 | convolution fusion | flops 1692819456 | bytes 7995938 | tf_op jit(solution)/shard_map/hts,shd->thd/dot_general | solution.py:86
  118.0 1.1 slice.46
  119.4 10.6 %fusion.45 = (f32[2,1024]{1,0:T(2,128)S(1)}, f32[2,1024,1088]{1,2,0:T(8,128)}) fusion(f32[1024,1088]{0,1:T(8,128)} %get-tuple-element.58, pred[1024,1088]{0,1:T(8,128)(4,1)} %get-tuple-element.57, bf16[1024,2,2,128]{0,3,2,1:T(8,128)(2,1)} %bitcast.86, bf16[1024,2,128]{2,0,1:T(8,128)(2,1)S(1)} %bitcast.82, bf16[64,2,128]{2,0,1:T(8,128)(2,1)S(1)} %collective-permute-done.2), kind=kOutput, calls=%fused_computation.77 | convolution fusion | flops 582681664 | bytes 15572992 | tf_op jit(solution)/shard_map/sub | solution.py:128
  130.0 7.5 %all-gather.7.cloned.1.call-done = bf16[32,273,128]{2,1,0:T(8,128)(2,1)} async-done(((bf16[2,273,128]{2,1,0:T(8,128)(2,1)}), bf16[32,273,128]{2,1,0:T(8,128)(2,1)}) %all-gather.7.cloned.1.call-update) | async-done | bytes 2236432 | tf_op jit(solution)/shard_map/all_gather | solution.py:14
  137.5 14.7 %while.12 = (s32[]{:T(128)}, f32[2,273,128]{2,1,0:T(8,128)S(1)}, f32[1]{0:T(128)}, s32[]{:T(128)}, bf16[16,1]{0,1:T(2,128)(2,1)S(1)}, /*index=5*/bf16[16,2,273,1...) while((s32[]{:T(128)}, f32[2,273,128]{2,1,0:T(8,128)S(1)}, f32[1]{0:T(128)}, s32[]{:T(128)}, ...), condition=%wide.region_1.2_spmd, body=%wide.region_0.1_spmd.sunk | while | flops 279560 | bytes 699054 | solution.py:28
  139.4 1.1 fusion.59
  143.1 1.1 fusion.59
  146.7 1.1 fusion.59
  150.3 1.1 fusion.59
  152.3 2.6 multiply_reduce_fusion
  154.9 4.6 %fusion.19 = bf16[1024,2,128]{0,2,1:T(8,128)(2,1)S(1)} fusion(f32[2,1024,1088]{1,2,0:T(8,128)} %get-tuple-element.60, f32[2,1024]{1,0:T(2,128)S(1)} %get-tuple-element.59, f32[1024,2,128]{0,2,1:T(8,128)S(1)} %get-tuple-element.62, bf16[1024,2,128]{2,0,1:T(8,128)(2,1)S(1)} %copy-done.7, bf16[64,2,128]{2,0,1:T(8,128)(2,1)} %collective-permute-done, ...), kind=kOutput, calls=%fused_computation.32 | convolution fusion | flops 576782336 | bytes 11059200 | tf_op jit(solution)/shard_map/hts,shd->thd/dot_general | solution.py:130
  159.5 5.6 %convert_bitcast_fusion = bf16[4096,1024]{0,1:T(8,128)(2,1)} fusion(bf16[1024,256]{0,1:T(8,128)(2,1)S(1)} %bitcast.83, bf16[256,4096]{1,0:T(8,128)(2,1)S(1)} %copy-done), kind=kOutput, calls=%fused_computation.7 | convolution fusion | flops 2151677952 | bytes 11010048 | tf_op jit(solution)/shard_map/dot_general | solution.py:133
  165.2 109.8 %reduce-scatter.2.cloned.1.call-done = bf16[256,1024]{0,1:T(8,128)(2,1)} async-done(((bf16[4096,1024]{0,1:T(8,128)(2,1)}), bf16[256,1024]{0,1:T(8,128)(2,1)}) %reduce-scatter.2.cloned.1.call-update) | async-done | bytes 524304 | tf_op jit(solution)/shard_map/reduce_scatter | solution.py:132
  (52 shorter events, 6.3 us)
Async XLA Ops:
  6.5 153.0 %copy-start = (bf16[256,4096]{1,0:T(8,128)(2,1)S(1)}, bf16[256,4096]{1,0:T(8,128)(2,1)}, u32[]{:S(2)}) copy-start(bf16[256,4096]{1,0:T(8,128)(2,1)} %param.13) | copy-start | bytes 6291460
  6.5 69.6 %copy-start.6 = (bf16[4096,64]{0,1:T(8,128)(2,1)S(1)}, bf16[4096,64]{0,1:T(8,128)(2,1)}, u32[]{:S(2)}) copy-start(bf16[4096,64]{0,1:T(8,128)(2,1)} %param.10) | copy-start | bytes 1572868
  6.5 69.6 %all-gather.5.cloned.1.call-start = ((), (), s32[]{:S(2)}) async-start(), calls=%async_computation.1 | async-start | bytes 8912896 | tf_op jit(solution)/shard_map/all_gather | solution.py:65
  7.3 130.2 %all-gather.7.cloned.1.call-start = ((), (), s32[]{:S(2)}) async-start(), calls=%async_computation.3 | async-start | bytes 2437120 | tf_op jit(solution)/shard_map/all_gather | solution.py:14
  11.2 77.1 %collective-permute-start.1 = (bf16[64]{0:T(256)(128)(2,1)S(1)}, bf16[64]{0:T(256)(128)(2,1)S(1)}, u32[]{:S(2)}, u32[]{:S(2)}) collective-permute-start(bf16[64]{0:T(256)(128)(2,1)S(1)} %add_convert_fusion), channel_id=1, source_target_pairs={{0,16},{16,32},{32,48},{48,64},{64,80},{80,96},{96,112},{112,128},... | collective-permute-start | bytes 392 | tf_op jit(solution)/shard_map/ppermute | solution.py:34
  76.1 6.8 %copy-start.1 = (bf16[1024,4096]{1,0:T(8,128)(2,1)S(1)}, bf16[1024,4096]{1,0:T(8,128)(2,1)}, u32[]{:S(2)}) copy-start(bf16[1024,4096]{1,0:T(8,128)(2,1)} %all-gather.5.cloned.1.call-done) | copy-start | bytes 25165828
  82.3 1.6 copy-start.11
  83.9 2.4 copy-start.4
  83.9 26.3 %copy-start.2 = (bf16[1024,2,16,16]{0,3,2,1:T(8,128)(2,1)}, bf16[1024,2,16,16]{0,3,2,1:T(8,128)(2,1)S(1)}, u32[]{:S(2)}) copy-start(bf16[1024,2,16,16]{0,3,2,1:T(8,128)(2,1)S(1)} %get-tuple-element.64) | copy-start | bytes 3145732
  86.2 0.8 copy-start.5
  88.3 186.7 %reduce-scatter.2.cloned.1.call-start = ((), (), s32[]{:S(2)}) async-start(), calls=%async_computation.2 | async-start | bytes 8912896 | tf_op jit(solution)/shard_map/reduce_scatter | solution.py:132
  88.4 3.5 %copy-start.10 = (bf16[4096,512]{1,0:T(8,128)(2,1)S(1)}, bf16[4096,512]{1,0:T(8,128)(2,1)}, u32[]{:S(2)}) copy-start(bf16[4096,512]{1,0:T(8,128)(2,1)} %param.12) | copy-start | bytes 12582916
  99.3 1.0 copy-start.8
  100.5 18.9 %collective-permute-start.2 = (bf16[64,2,128]{2,0,1:T(8,128)(2,1)S(1)}, bf16[64,2,128]{2,0,1:T(8,128)(2,1)S(1)}, u32[]{:S(2)}, u32[]{:S(2)}) collective-permute-start(bf16[64,2,128]{2,0,1:T(8,128)(2,1)S(1)} %bitcast.88), channel_id=1, source_target_pairs={{0,16},{16,32},{32,48},{48,64},{64,80},{80,96},{96,112},{112,128},... | collective-permute-start | bytes 98312 | tf_op jit(solution)/shard_map/ppermute | solution.py:34
  104.7 50.3 %collective-permute-start = (bf16[64,2,128]{2,0,1:T(8,128)(2,1)S(1)}, bf16[64,2,128]{2,0,1:T(8,128)(2,1)}, u32[]{:S(2)}, u32[]{:S(2)}) collective-permute-start(bf16[64,2,128]{2,0,1:T(8,128)(2,1)S(1)} %copy_bitcast_fusion.1), channel_id=1, source_target_pairs={{0,16},{16,32},{32,48},{48,64},{64,80},{80,96},{96,112},{112,128},... | collective-permute-start | bytes 98312 | tf_op jit(solution)/shard_map/ppermute | solution.py:34
  129.9 22.3 %copy-start.9 = (s32[1024]{0:T(1024)S(1)}, s32[1024]{0:T(1024)}, u32[]{:S(2)}) copy-start(s32[1024]{0:T(1024)} %param.9) | copy-start | bytes 12292
  130.0 22.3 %copy-start.3 = (bf16[1024,2,16,16]{0,3,2,1:T(8,128)(2,1)S(1)}, bf16[1024,2,16,16]{0,3,2,1:T(8,128)(2,1)}, u32[]{:S(2)}) copy-start(bf16[1024,2,16,16]{0,3,2,1:T(8,128)(2,1)} %copy-done.2) | copy-start | bytes 3145732
  152.3 2.7 copy-start.7
Sparse Core Ops, SparseCore 0:
  9.1 66.9 all-gather.4
  88.4 49.0 all-gather.6
  165.3 109.6 reduce-scatter.1
where the time goes:
time: 283 us; the launch traced here: 282 us
  waiting for transfers between devices  142 us (50%)
  matrix products  48.2 us (17%)
  blocking collectives  33.2 us (12%)
  between operations  13.4 us (5%)
  local copies, waits for them, and re-layouts  13.2 us (5%)
  other arithmetic  13.1 us (5%)
  starting transfers between devices  10.5 us (4%)
  loops' own time  8.18 us (3%)
    reduce_scatter x1, waiting for transfers between devices, shards(): lax.psum_scatter(lax.dot_general(w_out, mixed, (((0,), (1,)), ((), ())),...  110 us
    unnamed x1, blocking collectives  33.2 us
    all_gather x1, waiting for transfers between devices, shards(): column_piece = lax.all_gather(tokens, 'head', axis=1, tiled=True)  23.7 us
    dot_general x3, matrix products, shards(): jnp.dot(column_piece, weight, preferred_element_type=jnp.float32)  15.8 us
    sub x1, matrix products, shards(): weights = jnp.exp(logits - top_logit) * within[None].astype(jnp.float32)  10.6 us
    ppermute x3, starting transfers between devices, shifted(): return lax.ppermute(x, axis, pairs)  10.4 us
    another operation x1, loops' own time, entering(): return lax.fori_loop(0, place, one, state)  8.18 us
    dot_general x1, matrix products, shards(): jnp.einsum('hts,shd->thd', scores, values_here, preferred_element_type=jn...  7.79 us
  transfers between devices with their start and end apart: 6, of which 3 were waited for; matrix products, arithmetic and copies ran while one was open for 22% of the time, Pallas kernels for 0%

commit v1 on v0

--- a/solution.py
+++ b/solution.py
@@ -62,7 +62,9 @@
         jnp.zeros((tok_rows, w_value.shape[1]), jnp.float32),
         jnp.zeros((tok_rows, w_window.shape[1]), jnp.float32),
     )
-    column_piece = lax.all_gather(tokens, "head", axis=1, tiled=True)
+    column_piece = jnp.concatenate(
+        lax.all_to_all(jnp.stack([tokens] * lax.axis_size("head")), "head", 0, 0), axis=1
+    )
     updated = []
     for running, weight in zip(zero_sums, (w_feat, w_value, w_window)):
         updated.append(jnp.dot(column_piece, weight, preferred_element_type=jnp.float32))

time: 283 us -> 432 us (1.53)
  waiting for transfers between devices: 142 us -> 280 us
  starting transfers between devices: 10.5 us -> 16.5 us
    all_to_all x0 -> x1, waiting for transfers between devices: none -> 174 us  [shards(): lax.all_to_all(jnp.stack([tokens] * lax.axis_size('head')), 'head', 0, 0)]
    all_gather x1 -> x0, waiting for transfers between devices: 23.7 us -> none  [shards(): column_piece = lax.all_gather(tokens, 'head', axis=1, tiled=True)]
    all_to_all x0 -> x1, starting transfers between devices: none -> 8.75 us  [shards(): lax.all_to_all(jnp.stack([tokens] * lax.axis_size('head')), 'head', 0, 0)]
    all_gather x1, waiting for transfers between devices: 7.53 us -> 0.01 us  [entering(): lax.all_gather(a.astype(kind), axis)]
  transfers between devices with their start and end apart: 6 -> 6, of which waited for: 3 -> 2; matrix products, arithmetic and copies ran while one was open for 22% -> 14% of each run, Pallas kernels for 0% -> 0%
where the time goes in v1:
time: 432 us; the launch traced here: 431 us
  waiting for transfers between devices  280 us (65%)
  matrix products  50.7 us (12%)
  blocking collectives  34.8 us (8%)
  starting transfers between devices  16.5 us (4%)
  local copies, waits for them, and re-layouts  15.5 us (4%)
  between operations  13.7 us (3%)
  other arithmetic  12.7 us (3%)
  loops' own time  7.25 us (2%)
    all_to_all x1, waiting for transfers between devices, shards(): lax.all_to_all(jnp.stack([tokens] * lax.axis_size('head')), 'head', 0, 0)  174 us
    reduce_scatter x1, waiting for transfers between devices, shards(): lax.psum_scatter(lax.dot_general(w_out, mixed, (((0,), (1,)), ((), ())),...  106 us
    unnamed x1, blocking collectives  34.8 us
    dot_general x3, matrix products, shards(): jnp.dot(column_piece, weight, preferred_element_type=jnp.float32)  18.2 us
    sub x1, matrix products, shards(): weights = jnp.exp(logits - top_logit) * within[None].astype(jnp.float32)  10.6 us
    all_to_all x1, starting transfers between devices, shards(): lax.all_to_all(jnp.stack([tokens] * lax.axis_size('head')), 'head', 0, 0)  8.75 us
  transfers between devices with their start and end apart: 6, of which 2 were waited for; matrix products, arithmetic and copies ran while one was open for 14% of the time, Pallas kernels for 0%

profile of v1, /device:TPU:2, one launch (start us, length us, event | category | flops | bytes accessed | tf_op | source)
XLA Modules:
  0.0 431.2 jit_solution(17886107794129457957)
XLA Ops:
  6.5 1.4 copy.22
  7.9 4.3 stack.2
  12.2 8.8 %all-to-all-start = ((bf16[16,1024,256]{1,2,0:T(8,128)(2,1)}), bf16[16,1024,256]{1,2,0:T(8,128)(2,1)}, u32[]{:S(2)}, u32[]{:S(2)}) async-start(bf16[16,1024,256]{1,2,0:T(8,128)(2,1)} %stack.2), calls=%async_computation | async-start | bytes 16777216 | tf_op jit(solution)/shard_map/all_to_all | solution.py:66
  21.2 3.6 collective-permute-start.1
  24.8 0.6 slice.34
  26.6 1.3 dynamic-update-slice
  28.5 2.5 fusion.12
  31.1 174.1 %all-to-all-done = bf16[16,1024,256]{1,2,0:T(8,128)(2,1)} async-done(((bf16[16,1024,256]{1,2,0:T(8,128)(2,1)}), bf16[16,1024,256]{1,2,0:T(8,128)(2,1)}, u32[]{:S(2)}, u32[]{:S(2)}) %all-to-all-start) | async-done | bytes 8388640 | tf_op jit(solution)/shard_map/all_to_all | solution.py:66
  205.2 5.1 %convolution_convert_fusion.3 = bf16[1024,64]{0,1:T(8,128)(2,1)S(1)} fusion(bf16[4096,64]{0,1:T(8,128)(2,1)S(1)} %copy-done.2, bf16[1024,4096]{0,1:T(8,128)(2,1)} %bitcast.6), kind=kOutput, calls=%fused_computation.36 | convolution fusion | flops 536936448 | bytes 9043968 | tf_op jit(solution)/shard_map/dot_general | solution.py:70
  210.4 5.8 %convolution_convert_fusion.1 = bf16[1024,256]{1,0:T(8,128)(2,1)S(1)} fusion(bf16[1024,4096]{0,1:T(8,128)(2,1)} %bitcast.6, bf16[4096,256]{1,0:T(8,128)(2,1)S(1)} %copy-done.1), kind=kOutput, calls=%fused_computation.33 | convolution fusion | flops 2147745792 | bytes 11010048 | tf_op jit(solution)/shard_map/dot_general | solution.py:70
  216.2 1.5 multiply_convert_fusion.2
  217.7 1.0 copy-done.4
  218.7 1.2 convolution_convert_fusion.2
  220.0 34.8 %all-reduce = bf16[16]{0:T(256)(128)(2,1)S(1)} all-reduce(bf16[16]{0:T(256)(128)(2,1)S(1)} %dynamic-update-slice), channel_id=2, replica_groups=mesh['ctx'=16,'head'=16] {'ctx'}, use_global_device_ids=true, to_apply=%add | all-reduce | flops 16 | bytes 64
  254.8 3.6 fusion.6
  258.4 7.3 %convolution_convert_fusion = bf16[1024,512]{0,1:T(8,128)(2,1)S(1)} fusion(bf16[1024,4096]{0,1:T(8,128)(2,1)} %bitcast.6, bf16[4096,512]{1,0:T(8,128)(2,1)S(1)} %copy-done.8), kind=kOutput, calls=%fused_computation.26 | convolution fusion | flops 4295491584 | bytes 13631488 | tf_op jit(solution)/shard_map/dot_general | solution.py:70
  265.7 1.0 copy-done.6
  266.9 1.9 collective-permute-start.2
  268.9 2.1 collective-permute-start
  271.0 0.8 copy_bitcast_fusion
  271.8 7.9 %fusion.9 = f32[2,128,1024]{2,1,0:T(8,128)} fusion(f32[1024,1024]{1,0:T(8,128)} %fusion.12, bf16[1024,2,256]{0,2,1:T(8,128)(2,1)} %bitcast.84, bf16[1024,2,16]{0,2,1:T(8,128)(2,1)S(1)} %get-tuple-element.54, bf16[1024,2,256]{0,2,1:T(8,128)(2,1)} %bitcast.81, bf16[1024,2,16]{0,2,1:T(8,128)(2,1)S(1)} %get-tuple-element.53, bf16[273]{0:T(512)(128)(2,1)S(1)} %pad.9.clone, ...), kind=kOutput, calls=%fused_computation.18 | convolution fusion | flops 1692819456 | bytes 7995938 | tf_op jit(solution)/shard_map/hts,shd->thd/dot_general | solution.py:88
  279.8 1.1 slice.46
  281.1 10.6 %fusion.45 = (f32[2,1024]{1,0:T(2,128)S(1)}, f32[2,1024,1088]{1,2,0:T(8,128)}) fusion(f32[1024,1088]{0,1:T(8,128)} %get-tuple-element.58, pred[1024,1088]{0,1:T(8,128)(4,1)} %get-tuple-element.57, bf16[1024,2,2,128]{0,3,2,1:T(8,128)(2,1)} %bitcast.89, bf16[1024,2,128]{2,0,1:T(8,128)(2,1)S(1)} %bitcast.85, bf16[64,2,128]{2,0,1:T(8,128)(2,1)S(1)} %collective-permute-done.2), kind=kOutput, calls=%fused_computation.77 | convolution fusion | flops 582681664 | bytes 15572992 | tf_op jit(solution)/shard_map/sub | solution.py:130
  291.7 13.7 %while.12 = (s32[]{:T(128)}, f32[2,273,128]{2,1,0:T(8,128)S(1)}, f32[1]{0:T(128)}, s32[]{:T(128)}, bf16[16,1]{0,1:T(2,128)(2,1)S(1)}, /*index=5*/bf16[16,2,273,1...) while((s32[]{:T(128)}, f32[2,273,128]{2,1,0:T(8,128)S(1)}, f32[1]{0:T(128)}, s32[]{:T(128)}, ...), condition=%wide.region_1.2_spmd, body=%wide.region_0.1_spmd.sunk | while | flops 279560 | bytes 699054 | solution.py:28
  293.4 1.1 fusion.59
  296.8 1.1 fusion.59
  300.2 1.1 fusion.59
  303.6 1.1 fusion.59
  305.5 2.6 multiply_reduce_fusion
  308.1 4.6 %fusion.19 = bf16[1024,2,128]{0,2,1:T(8,128)(2,1)S(1)} fusion(f32[2,1024,1088]{1,2,0:T(8,128)} %get-tuple-element.60, f32[2,1024]{1,0:T(2,128)S(1)} %get-tuple-element.59, f32[1024,2,128]{0,2,1:T(8,128)S(1)} %get-tuple-element.62, bf16[1024,2,128]{2,0,1:T(8,128)(2,1)S(1)} %copy-done.5, bf16[64,2,128]{2,0,1:T(8,128)(2,1)} %collective-permute-done, ...), kind=kOutput, calls=%fused_computation.32 | convolution fusion | flops 576782336 | bytes 11059200 | tf_op jit(solution)/shard_map/hts,shd->thd/dot_general | solution.py:132
  312.7 5.6 %convert_bitcast_fusion = bf16[4096,1024]{0,1:T(8,128)(2,1)} fusion(bf16[1024,256]{0,1:T(8,128)(2,1)S(1)} %bitcast.86, bf16[256,4096]{1,0:T(8,128)(2,1)S(1)} %copy-done), kind=kOutput, calls=%fused_computation.7 | convolution fusion | flops 2151677952 | bytes 11010048 | tf_op jit(solution)/shard_map/dot_general | solution.py:135
  318.4 106.0 %reduce-scatter.2.cloned.1.call-done = bf16[256,1024]{0,1:T(8,128)(2,1)} async-done(((bf16[4096,1024]{0,1:T(8,128)(2,1)}), bf16[256,1024]{0,1:T(8,128)(2,1)}) %reduce-scatter.2.cloned.1.call-update) | async-done | bytes 524304 | tf_op jit(solution)/shard_map/reduce_scatter | solution.py:134
  (49 shorter events, 4.9 us)
Async XLA Ops:
  6.5 306.2 %copy-start = (bf16[256,4096]{1,0:T(8,128)(2,1)S(1)}, bf16[256,4096]{1,0:T(8,128)(2,1)}, u32[]{:S(2)}) copy-start(bf16[256,4096]{1,0:T(8,128)(2,1)} %param.13) | copy-start | bytes 6291460
  12.2 8.8 %copy-start.7 = (s32[1024]{0:T(1024)S(1)}, s32[1024]{0:T(1024)}, u32[]{:S(2)}) copy-start(s32[1024]{0:T(1024)} %param.9) | copy-start | bytes 12292
  12.2 13.8 %copy-start.9 = (u32[256]{0:T(256)S(1)}, u32[256]{0:T(256)}, u32[]{:S(2)}) copy-start(u32[256]{0:T(256)} %constant.58) | copy-start | bytes 3076
  12.2 193.0 %all-to-all-start = ((bf16[16,1024,256]{1,2,0:T(8,128)(2,1)}), bf16[16,1024,256]{1,2,0:T(8,128)(2,1)}, u32[]{:S(2)}, u32[]{:S(2)}) async-start(bf16[16,1024,256]{1,2,0:T(8,128)(2,1)} %stack.2), calls=%async_computation | async-start | bytes 16777216 | tf_op jit(solution)/shard_map/all_to_all | solution.py:66
  21.0 184.2 %copy-start.2 = (bf16[4096,64]{0,1:T(8,128)(2,1)S(1)}, bf16[4096,64]{0,1:T(8,128)(2,1)}, u32[]{:S(2)}) copy-start(bf16[4096,64]{0,1:T(8,128)(2,1)} %param.10) | copy-start | bytes 1572868
  21.0 270.7 %all-gather.4.cloned.1.call-start = ((), (), s32[]{:S(2)}) async-start(), calls=%async_computation.3 | async-start | bytes 2437120 | tf_op jit(solution)/shard_map/all_gather | solution.py:14
  21.2 233.6 %collective-permute-start.1 = (bf16[64]{0:T(256)(128)(2,1)S(1)}, bf16[64]{0:T(256)(128)(2,1)S(1)}, u32[]{:S(2)}, u32[]{:S(2)}) collective-permute-start(bf16[64]{0:T(256)(128)(2,1)S(1)} %add_convert_fusion), channel_id=1, source_target_pairs={{0,16},{16,32},{32,48},{48,64},{64,80},{80,96},{96,112},{112,128},... | collective-permute-start | bytes 392 | tf_op jit(solution)/shard_map/ppermute | solution.py:34
  205.2 5.2 %copy-start.1 = (bf16[4096,256]{1,0:T(8,128)(2,1)S(1)}, bf16[4096,256]{1,0:T(8,128)(2,1)}, u32[]{:S(2)}) copy-start(bf16[4096,256]{1,0:T(8,128)(2,1)} %param.11) | copy-start | bytes 6291460
  217.7 1.0 copy-start.4
  219.9 204.5 %reduce-scatter.2.cloned.1.call-start = ((), (), s32[]{:S(2)}) async-start(), calls=%async_computation.2 | async-start | bytes 8912896 | tf_op jit(solution)/shard_map/reduce_scatter | solution.py:134
  254.8 3.6 copy-start.8
  265.7 1.0 copy-start.6
  266.9 14.2 %collective-permute-start.2 = (bf16[64,2,128]{2,0,1:T(8,128)(2,1)S(1)}, bf16[64,2,128]{2,0,1:T(8,128)(2,1)S(1)}, u32[]{:S(2)}, u32[]{:S(2)}) collective-permute-start(bf16[64,2,128]{2,0,1:T(8,128)(2,1)S(1)} %bitcast.91), channel_id=1, source_target_pairs={{0,16},{16,32},{32,48},{48,64},{64,80},{80,96},{96,112},{112,128},... | collective-permute-start | bytes 98312 | tf_op jit(solution)/shard_map/ppermute | solution.py:34
  268.9 39.2 %collective-permute-start = (bf16[64,2,128]{2,0,1:T(8,128)(2,1)S(1)}, bf16[64,2,128]{2,0,1:T(8,128)(2,1)}, u32[]{:S(2)}, u32[]{:S(2)}) collective-permute-start(bf16[64,2,128]{2,0,1:T(8,128)(2,1)S(1)} %copy_bitcast_fusion.1), channel_id=1, source_target_pairs={{0,16},{16,32},{32,48},{48,64},{64,80},{80,96},{96,112},{112,128},... | collective-permute-start | bytes 98312 | tf_op jit(solution)/shard_map/ppermute | solution.py:34
  291.7 13.8 %copy-start.3 = (bf16[1024,2,16,16]{0,3,2,1:T(8,128)(2,1)S(1)}, bf16[1024,2,16,16]{0,3,2,1:T(8,128)(2,1)}, u32[]{:S(2)}) copy-start(bf16[1024,2,16,16]{0,3,2,1:T(8,128)(2,1)} %get-tuple-element.64) | copy-start | bytes 3145732
  305.4 2.7 copy-start.5
Sparse Core Ops, SparseCore 0:
  220.0 49.1 all-gather.3
  318.5 105.8 reduce-scatter.1
